TPU v7x, 32 devices: a whole 2x2x4 slice. The times are simulated.
32 devices in a mesh: seq: 4 (over x, core), fsdp: 8 (over z, y).
Axes of the slice: x: 2, y: 2, z: 4, core: 2. Of those that a mesh axis runs over, the one named last changes fastest.
Arguments:
- hidden_in: bfloat16 [8, 1024, 1536], P('fsdp', 'seq'), may hold values from -6 to 6
- positions: int32 [8, 1024], P('fsdp', 'seq'), may hold values from 0 to 5116, as said below
- attn_gain: bfloat16 [1536], P('fsdp'), may hold values from 0.25 to 1.75
- qkv_weight: bfloat16 [1536, 2048], P('fsdp'), may hold values from -0.15625 to 0.15625
- qkv_bias: bfloat16 [2048], P('fsdp'), may hold values from -3 to 3
- out_weight: bfloat16 [1536, 1536], P('fsdp'), may hold values from -1.75 to 1.75
- mlp_gain: bfloat16 [1536], P('fsdp'), may hold values from 0.25 to 1.75
- gate_weight: bfloat16 [8960, 1536], P('fsdp'), may hold values from -0.15625 to 0.15625
- up_weight: bfloat16 [8960, 1536], P('fsdp'), may hold values from -0.15625 to 0.15625
- down_weight: bfloat16 [8960, 1536], P('fsdp'), may hold values from -0.0625 to 0.0625
- cotangent: bfloat16 [8, 1024, 1536], P('fsdp', 'seq'), may hold values from -6 to 6
Outputs:
- hidden_out: bfloat16 [8, 1024, 1536], P('fsdp', 'seq')
- grad_in: float32 [8, 1024, 1536], P('fsdp', 'seq')
- grad_attn_gain: float32 [1536], P('fsdp')
- grad_qkv_weight: float32 [1536, 2048], P('fsdp')
- grad_qkv_bias: float32 [2048], P('fsdp')
- grad_out_weight: float32 [1536, 1536], P('fsdp')
- grad_mlp_gain: float32 [1536], P('fsdp')
- grad_gate_weight: float32 [8960, 1536], P('fsdp')
- grad_up_weight: float32 [8960, 1536], P('fsdp')
- grad_down_weight: float32 [8960, 1536], P('fsdp')
Inputs may be any that keep to these rules, and one draw needn't show every extreme that they name: Along each sequence the positions rise by 1 to 3 from one token to the next; the first lies below 2048.
All inputs are finite; a program needn't handle non-finite values.
Results may differ from a plain program's by a relative error of at most 0.019.
Values may be sent and summed in bfloat16 or wider, within the bound.
A program may use at most 320 MiB of HBM per device.

v0:
```python
import math
import jax
import jax.numpy as jnp
from jax import lax
from jax.sharding import PartitionSpec as P

HEADS = 12
KV_HEADS = 2
HEAD_DIM = 128
norm_eps = 1e-06
rope_base = 1000000.0


def rope_tables(position_row):
    half_dim = HEAD_DIM // 2
    frequency = jnp.exp(
        -(jnp.arange(half_dim, dtype=jnp.float32) * 2.0 / HEAD_DIM) * math.log(rope_base)
    )
    angles = position_row.astype(jnp.float32)[:, None] * frequency[None, :]
    angles = jnp.concatenate([angles, angles], axis=-1)
    return (jnp.cos(angles), jnp.sin(angles))


def rotate(values, cosine, sine):
    half_dim = values.shape[-1] // 2
    turned = jnp.concatenate([-values[..., half_dim:], values[..., :half_dim]], axis=-1)
    return values * cosine[:, None, :] + turned * sine[:, None, :]


def unrotate(grads_rot, cosine, sine):
    half_dim = grads_rot.shape[-1] // 2
    scaled = grads_rot * sine[:, None, :]
    return grads_rot * cosine[:, None, :] + jnp.concatenate(
        [scaled[..., half_dim:], -scaled[..., :half_dim]], axis=-1
    )


def norm_forward(values, gain):
    inverse = lax.rsqrt(jnp.mean(values * values, axis=-1, keepdims=True) + norm_eps)
    unit_rows = values * inverse
    return (unit_rows, inverse, (unit_rows * gain).astype(jnp.bfloat16))


def norm_backward(grad_normed, unit_rows, inverse, gain):
    grad_unit = grad_normed * gain
    grad_values = inverse * (
        grad_unit - unit_rows * jnp.mean(grad_unit * unit_rows, axis=-1, keepdims=True)
    )
    grad_gain = jnp.sum(grad_normed * unit_rows, axis=0)
    return (grad_values, grad_gain)


def masked_scores(queries, keys, block_start, block_rows):
    length = keys.shape[0]
    query_block = lax.dynamic_slice_in_dim(queries, block_start, block_rows, 0)
    scores = jnp.einsum(
        "bhd,ld->hbl", query_block, keys, preferred_element_type=jnp.float32
    ) * HEAD_DIM ** (-0.5)
    row_index = block_start + jnp.arange(block_rows)
    column_index = jnp.arange(length)
    allowed = column_index[None, :] <= row_index[:, None]
    return (query_block, jnp.where(allowed[None], scores, -1e30))


def attend_forward(queries, keys, values):
    length = keys.shape[0]
    block_rows = min(512, length)
    block_count = length // block_rows

    def one_block(block_start):
        query_block, scores = masked_scores(queries, keys, block_start, block_rows)
        row_max = jnp.max(scores, axis=-1, keepdims=True)
        exponent = jnp.exp(scores - row_max)
        row_total = jnp.sum(exponent, axis=-1, keepdims=True)
        probability = (exponent / row_total).astype(jnp.bfloat16)
        result = jnp.einsum("hbl,ld->bhd", probability, values, preferred_element_type=jnp.float32)
        return (result.astype(jnp.bfloat16), (row_max + jnp.log(row_total))[..., 0])

    results, log_totals = lax.map(one_block, jnp.arange(block_count) * block_rows)
    return (results.reshape(length, queries.shape[1], queries.shape[2]), log_totals)


def attend_backward(queries, keys, values, log_totals, grad_out):
    length = keys.shape[0]
    block_rows = min(512, length)
    block_count = length // block_rows
    score_scale = HEAD_DIM ** (-0.5)

    def one_block(running, inputs):
        grad_keys, grad_values = running
        block_start, log_block = inputs
        query_block, scores = masked_scores(queries, keys, block_start, block_rows)
        grad_block = lax.dynamic_slice_in_dim(grad_out, block_start, block_rows, 0)
        probability = jnp.exp(scores - log_block[..., None])
        grad_probs = jnp.einsum(
            "bhd,ld->hbl", grad_block, values, preferred_element_type=jnp.float32
        )
        row_delta = jnp.sum(probability * grad_probs, axis=-1, keepdims=True)
        grad_scores = (probability * (grad_probs - row_delta)).astype(jnp.bfloat16)
        grad_query = (
            jnp.einsum("hbl,ld->bhd", grad_scores, keys, preferred_element_type=jnp.float32)
            * score_scale
        )
        grad_keys = (
            grad_keys
            + jnp.einsum(
                "hbl,bhd->ld", grad_scores, query_block, preferred_element_type=jnp.float32
            )
            * score_scale
        )
        grad_values = grad_values + jnp.einsum(
            "hbl,bhd->ld",
            probability.astype(jnp.bfloat16),
            grad_block,
            preferred_element_type=jnp.float32,
        )
        return ((grad_keys, grad_values), grad_query)

    zero_rows = jnp.zeros((length, keys.shape[1]), jnp.float32)
    (grad_keys, grad_values), grad_query = lax.scan(
        one_block, (zero_rows, zero_rows), (jnp.arange(block_count) * block_rows, log_totals)
    )
    return (grad_query.reshape(queries.shape), grad_keys, grad_values)


def per_device(
    hidden_in,
    positions,
    attn_gain,
    qkv_weight,
    qkv_bias,
    out_weight,
    mlp_gain,
    gate_weight,
    up_weight,
    down_weight,
    cotangent,
):
    groups = lax.axis_size("seq")
    group_heads = HEADS // groups
    repeat = groups // KV_HEADS
    tokens = hidden_in.shape[1]
    width_query = HEADS * HEAD_DIM
    width_key = KV_HEADS * HEAD_DIM
    residual = hidden_in[0].astype(jnp.float32)
    cosine, sine = rope_tables(positions[0])
    gains_one, gains_two, qkv_full, bias_full, out_full = (
        lax.all_gather(attn_gain, "fsdp", axis=0, tiled=True),
        lax.all_gather(mlp_gain, "fsdp", axis=0, tiled=True),
        lax.all_gather(qkv_weight, "fsdp", axis=0, tiled=True),
        lax.all_gather(qkv_bias, "fsdp", axis=0, tiled=True),
        lax.all_gather(out_weight, "fsdp", axis=0, tiled=True),
    )
    gain_one = gains_one.astype(jnp.float32)
    gain_two = gains_two.astype(jnp.float32)
    unit_one, inverse_one, normed_one = norm_forward(residual, gain_one)
    qkv_mixed = jnp.dot(
        normed_one, qkv_full, preferred_element_type=jnp.float32
    ) + bias_full.astype(jnp.float32)
    query_part = qkv_mixed[:, :width_query].reshape(tokens, HEADS, HEAD_DIM)
    key_part = qkv_mixed[:, width_query : width_query + width_key].reshape(
        tokens, KV_HEADS, HEAD_DIM
    )
    value_part = qkv_mixed[:, width_query + width_key :].reshape(tokens, KV_HEADS, HEAD_DIM)
    queries = (
        rotate(query_part, cosine, sine)
        .astype(jnp.bfloat16)
        .reshape(tokens, groups, group_heads * HEAD_DIM)
    )
    keys_rep = jnp.repeat(rotate(key_part, cosine, sine).astype(jnp.bfloat16), repeat, axis=1)
    values_rep = jnp.repeat(value_part.astype(jnp.bfloat16), repeat, axis=1)
    head_queries, head_keys, head_values = (
        lax.all_to_all(queries, "seq", split_axis=1, concat_axis=0, tiled=True),
        lax.all_to_all(keys_rep, "seq", split_axis=1, concat_axis=0, tiled=True),
        lax.all_to_all(values_rep, "seq", split_axis=1, concat_axis=0, tiled=True),
    )
    head_queries = head_queries.reshape(-1, group_heads, HEAD_DIM)
    head_keys = head_keys.reshape(-1, HEAD_DIM)
    head_values = head_values.reshape(-1, HEAD_DIM)
    attended, log_totals = attend_forward(head_queries, head_keys, head_values)
    returned = lax.all_to_all(
        attended.reshape(-1, 1, group_heads * HEAD_DIM),
        "seq",
        split_axis=0,
        concat_axis=1,
        tiled=True,
    )
    attn_rows = returned.reshape(tokens, width_query)
    residual_two = residual + jnp.dot(attn_rows, out_full, preferred_element_type=jnp.float32)
    unit_two, inverse_two, normed_two = norm_forward(residual_two, gain_two)
    grad_output = cotangent[0].astype(jnp.float32)
    grad_mlp = grad_output.astype(jnp.bfloat16)
    all_rows = lax.all_gather(normed_two, "fsdp", axis=0, tiled=True)
    gate_pre = jnp.einsum("td,fd->tf", all_rows, gate_weight, preferred_element_type=jnp.float32)
    up_pre = jnp.einsum("td,fd->tf", all_rows, up_weight, preferred_element_type=jnp.float32)
    sigmoid_gate = jax.nn.sigmoid(gate_pre)
    activated = gate_pre * sigmoid_gate
    hidden = (activated * up_pre).astype(jnp.bfloat16)
    partial_out = jnp.dot(hidden, down_weight, preferred_element_type=jnp.float32)
    mlp_out = lax.psum_scatter(
        partial_out.astype(jnp.bfloat16), "fsdp", scatter_dimension=0, tiled=True
    ).astype(jnp.float32)
    all_grads = lax.all_gather(grad_mlp, "fsdp", axis=0, tiled=True)
    grad_hidden = jnp.einsum(
        "tm,fm->tf", all_grads, down_weight, preferred_element_type=jnp.float32
    )
    grad_gate = (
        grad_hidden * up_pre * sigmoid_gate * (1.0 + gate_pre * (1.0 - sigmoid_gate))
    ).astype(jnp.bfloat16)
    grad_up = (grad_hidden * activated).astype(jnp.bfloat16)
    partial_back = jnp.dot(grad_gate, gate_weight, preferred_element_type=jnp.float32) + jnp.dot(
        grad_up, up_weight, preferred_element_type=jnp.float32
    )
    grad_normed_two = lax.psum_scatter(partial_back, "fsdp", scatter_dimension=0, tiled=True)
    shard_gate = jnp.einsum("tf,td->fd", grad_gate, all_rows, preferred_element_type=jnp.float32)
    shard_up = jnp.einsum("tf,td->fd", grad_up, all_rows, preferred_element_type=jnp.float32)
    shard_down = jnp.einsum("tf,td->fd", hidden, all_grads, preferred_element_type=jnp.float32)
    hidden_out = (residual_two + mlp_out).astype(jnp.bfloat16)
    grad_norm_two, term_gain_two = norm_backward(grad_normed_two, unit_two, inverse_two, gain_two)
    grad_residual_two = grad_output + grad_norm_two
    grad_proj = grad_residual_two.astype(jnp.bfloat16)
    grad_attn_rows = jnp.einsum(
        "td,ed->te", grad_proj, out_full, preferred_element_type=jnp.float32
    ).astype(jnp.bfloat16)
    term_out = jnp.einsum("te,td->ed", attn_rows, grad_proj, preferred_element_type=jnp.float32)
    grad_heads = lax.all_to_all(
        grad_attn_rows.reshape(tokens, groups, group_heads * HEAD_DIM),
        "seq",
        split_axis=1,
        concat_axis=0,
        tiled=True,
    )
    grad_query, grad_keys, grad_values = attend_backward(
        head_queries,
        head_keys,
        head_values,
        log_totals,
        grad_heads.reshape(-1, group_heads, HEAD_DIM),
    )
    back_query, back_keys, back_values = (
        lax.all_to_all(
            grad_query.astype(jnp.bfloat16).reshape(-1, 1, group_heads * HEAD_DIM),
            "seq",
            split_axis=0,
            concat_axis=1,
            tiled=True,
        ),
        lax.all_to_all(
            grad_keys.astype(jnp.bfloat16)[:, None, :],
            "seq",
            split_axis=0,
            concat_axis=1,
            tiled=True,
        ),
        lax.all_to_all(
            grad_values.astype(jnp.bfloat16)[:, None, :],
            "seq",
            split_axis=0,
            concat_axis=1,
            tiled=True,
        ),
    )
    grad_query_rows = unrotate(
        back_query.reshape(tokens, HEADS, HEAD_DIM).astype(jnp.float32), cosine, sine
    )
    grad_key_rows = unrotate(
        jnp.sum(back_keys.astype(jnp.float32).reshape(tokens, KV_HEADS, repeat, HEAD_DIM), axis=2),
        cosine,
        sine,
    )
    grad_value_rows = jnp.sum(
        back_values.astype(jnp.float32).reshape(tokens, KV_HEADS, repeat, HEAD_DIM), axis=2
    )
    grad_mixed = jnp.concatenate(
        [
            grad_query_rows.reshape(tokens, width_query),
            grad_key_rows.reshape(tokens, width_key),
            grad_value_rows.reshape(tokens, width_key),
        ],
        axis=1,
    ).astype(jnp.bfloat16)
    term_qkv = jnp.einsum("td,tc->dc", normed_one, grad_mixed, preferred_element_type=jnp.float32)
    term_bias = jnp.sum(grad_mixed.astype(jnp.float32), axis=0)
    grad_normed_one = jnp.einsum(
        "tc,dc->td", grad_mixed, qkv_full, preferred_element_type=jnp.float32
    )
    grad_norm_one, term_gain_one = norm_backward(grad_normed_one, unit_one, inverse_one, gain_one)
    grad_rows = grad_residual_two + grad_norm_one
    shard_gain_one, shard_qkv, shard_bias, shard_out, shard_gain_two = (
        lax.psum_scatter(
            term_gain_one.astype(jnp.bfloat16), "fsdp", scatter_dimension=0, tiled=True
        ).astype(jnp.float32),
        lax.psum_scatter(
            term_qkv.astype(jnp.bfloat16), "fsdp", scatter_dimension=0, tiled=True
        ).astype(jnp.float32),
        lax.psum_scatter(
            term_bias.astype(jnp.bfloat16), "fsdp", scatter_dimension=0, tiled=True
        ).astype(jnp.float32),
        lax.psum_scatter(
            term_out.astype(jnp.bfloat16), "fsdp", scatter_dimension=0, tiled=True
        ).astype(jnp.float32),
        lax.psum_scatter(
            term_gain_two.astype(jnp.bfloat16), "fsdp", scatter_dimension=0, tiled=True
        ).astype(jnp.float32),
    )
    totals = (
        lax.psum(shard_gain_one.astype(jnp.bfloat16), "seq").astype(jnp.float32),
        lax.psum(shard_qkv.astype(jnp.bfloat16), "seq").astype(jnp.float32),
        lax.psum(shard_bias.astype(jnp.bfloat16), "seq").astype(jnp.float32),
        lax.psum(shard_out.astype(jnp.bfloat16), "seq").astype(jnp.float32),
        lax.psum(shard_gain_two.astype(jnp.bfloat16), "seq").astype(jnp.float32),
        lax.psum(shard_gate.astype(jnp.bfloat16), "seq").astype(jnp.float32),
        lax.psum(shard_up.astype(jnp.bfloat16), "seq").astype(jnp.float32),
        lax.psum(shard_down.astype(jnp.bfloat16), "seq").astype(jnp.float32),
    )
    return (
        hidden_out[None],
        grad_rows[None],
        totals[0],
        totals[1],
        totals[2],
        totals[3],
        totals[4],
        totals[5],
        totals[6],
        totals[7],
    )


def solution(mesh):
    placed = (
        P("fsdp", "seq", None),
        P("fsdp", "seq"),
        P("fsdp"),
        P("fsdp", None),
        P("fsdp"),
        P("fsdp", None),
        P("fsdp"),
        P("fsdp", None),
        P("fsdp", None),
        P("fsdp", None),
        P("fsdp", "seq", None),
    )
    return jax.shard_map(
        per_device,
        mesh=mesh,
        in_specs=placed,
        out_specs=(
            P("fsdp", "seq", None),
            P("fsdp", "seq", None),
            P("fsdp"),
            P("fsdp", None),
            P("fsdp"),
            P("fsdp", None),
            P("fsdp"),
            P("fsdp", None),
            P("fsdp", None),
            P("fsdp", None),
        ),
        check_vma=False,
    )
```

profile of v0, /device:TPU:0, one launch (start us, length us, event | category | flops | bytes accessed | tf_op | source)
XLA Modules:
  0.0 1280.1 jit_solution(13989524856095700904)
XLA Ops:
  12.4 23.9 %all-reduce.6 = (bf16[1536]{0:T(1024)(128)(2,1)S(1)}, bf16[1536]{0:T(1024)(128)(2,1)S(1)}) all-reduce(bf16[1536]{0:T(1024)(128)(2,1)S(1)} %dynamic-update-slice, bf16[1536]{0:T(1024)(128)(2,1)S(1)} %dynamic-update-slice.1), channel_id=1, replica_groups=mesh['seq'=4,'fsdp'=8] {'fsdp'}, use_global_device_ids=true, to_apply=%add | all-reduce | flops 3072 | bytes 12288
  38.4 16.5 %all-gather.1 = bf16[8,1,256]{2,1,0:T(2,128)(2,1)S(1)} all-gather(bf16[1,1,256]{2,1,0:T(2,128)(2,1)S(1)} %reshape.306), channel_id=1, replica_groups=mesh['seq'=4,'fsdp'=8] {'fsdp'}, dimensions={0}, use_global_device_ids=true | all-gather | bytes 4608 | tf_op jit(solution)/shard_map/all_gather | solution.py:151
  60.3 52.2 %all-gather.7.cloned.1.call-done = bf16[1536,2048]{1,0:T(8,128)(2,1)} async-done(((bf16[192,2048]{1,0:T(8,128)(2,1)}), bf16[1536,2048]{1,0:T(8,128)(2,1)}) %all-gather.7.cloned.1.call-update) | async-done | bytes 6291472 | tf_op jit(solution)/shard_map/all_gather | solution.py:150
  142.2 10.1 all-to-all-done
  165.9 23.9 %while.27 = (s32[]{:T(128)}, bf16[2,512,3,128]{3,1,2,0:T(8,128)(2,1)}, f32[2,3,512]{2,1,0:T(4,128)S(1)}, s32[2]{0:T(128)S(1)}, bf16[1024,3,128]{2,0,1:T(8,128)(2...) while((s32[]{:T(128)}, ...), condition=%wide.region_4.5_spmd, body=%wide.region_1.4_spmd.sunk | while | flops 824900608 | bytes 22342304 | solution.py:79
  192.6 5.6 reshape.319
  198.7 7.3 reduce.2
  212.2 11.7 all-to-all-done.3
  239.6 95.6 %all-gather.11.cloned.1.call-done = bf16[2048,1536]{1,0:T(8,128)(2,1)} async-done(((bf16[256,1536]{1,0:T(8,128)(2,1)}), bf16[2048,1536]{1,0:T(8,128)(2,1)}) %all-gather.11.cloned.1.call-update) | async-done | bytes 6291472 | tf_op jit(solution)/shard_map/all_gather | solution.py:193
  335.2 13.4 %fusion.80 = f32[2048,1120]{0,1:T(8,128)} fusion(bf16[2048,1536]{1,0:T(8,128)(2,1)} %all-gather.11.cloned.1.call-done, bf16[1120,1536]{1,0:T(8,128)(2,1)} %param.22), kind=kOutput, calls=%fused_computation.140 | convolution fusion | flops 7046430720 | bytes 18907136 | tf_op jit(solution)/shard_map/td,fd->tf/dot_general | solution.py:194
  348.6 9.6 fusion.81
  358.2 76.3 %all-gather.13.cloned.1.call-done = bf16[1,2048,1536]{2,1,0:T(8,128)(2,1)} async-done(((bf16[1,256,1536]{2,1,0:T(8,128)(2,1)}), bf16[1,2048,1536]{2,1,0:T(8,128)(2,1)}) %all-gather.13.cloned.1.call-update) | async-done | bytes 6291472 | tf_op jit(solution)/shard_map/all_gather | solution.py:203
  434.5 18.3 %multiply_convert_fusion = (bf16[2048,1120]{0,1:T(8,128)(2,1)}, bf16[2048,1120]{0,1:T(8,128)(2,1)}, bf16[2048,1120]{0,1:T(8,128)(2,1)}) fusion(f32[2048,1120]{0,1:T(8,128)} %fusion.80, f32[2048,1120]{0,1:T(8,128)} %fusion.81, bf16[1120,1536]{1,0:T(8,128)(2,1)S(1)} %copy-done, bf16[1,2048,1536]{2,1,0:T(8,128)(2,1)} %all-gather.13.cloned.1.call-done), kind=kOutput, calls=%fused_computation.56 | convolution fusion | flops 7080837120 | bytes 41844736 | tf_op jit(solution)/shard_map/tm,fm->tf/dot_general | solution.py:204
  452.8 13.0 %fusion.82 = f32[2048,1536]{1,0:T(8,128)} fusion(bf16[2048,1120]{0,1:T(8,128)(2,1)} %get-tuple-element.264, bf16[1120,1536]{1,0:T(8,128)(2,1)S(1)} %copy-done.31), kind=kOutput, calls=%fused_computation.142 | convolution fusion | flops 7046430720 | bytes 20611072 | tf_op jit(solution)/shard_map/dot_general | solution.py:211
  465.9 14.2 %convolution_add_fusion = f32[2048,1536]{1,0:T(8,128)} fusion(f32[2048,1536]{1,0:T(8,128)} %fusion.82, bf16[2048,1120]{0,1:T(8,128)(2,1)S(1)} %copy-done.34, bf16[1120,1536]{1,0:T(8,128)(2,1)S(1)} %copy-done.33), kind=kOutput, calls=%fused_computation.61 | convolution fusion | flops 7049576448 | bytes 33193984 | tf_op jit(solution)/shard_map/dot_general | solution.py:211
  480.1 12.4 convolution_convert_fusion
  492.6 193.1 %reduce-scatter.7.cloned.1.call-done = f32[256,1536]{1,0:T(8,128)} async-done(((f32[2048,1536]{1,0:T(8,128)}), f32[256,1536]{1,0:T(8,128)}) %reduce-scatter.7.cloned.1.call-update) | async-done | bytes 1572880 | tf_op jit(solution)/shard_map/reduce_scatter | solution.py:214
  688.2 118.6 %reduce-scatter.5.cloned.1.call-done = bf16[256,1536]{1,0:T(8,128)(2,1)} async-done(((bf16[2048,1536]{1,0:T(8,128)(2,1)}), bf16[256,1536]{1,0:T(8,128)(2,1)}) %reduce-scatter.5.cloned.1.call-update) | async-done | bytes 786448 | tf_op jit(solution)/shard_map/reduce_scatter | solution.py:200
  822.7 7.9 all-to-all-done.4
  831.8 46.7 %while.28 = (s32[]{:T(128)}, f32[1024,128]{1,0:T(8,128)}, f32[1024,128]{1,0:T(8,128)}, bf16[2,512,3,128]{3,1,2,0:T(8,128)(2,1)}, s32[2]{0:T(128)S(1)}, /*index=5...) while((s32[]{:T(128)}, f32[1024,128]{1,0:T(8,128)}, ...), condition=%wide.region_11.12_spmd.clone, body=%wide.region_9.11_spmd.clone.sunk | while | flops 2038234112 | bytes 90227544 | solution.py:120
  849.4 6.0 fusion.140
  872.6 6.0 fusion.140
  909.9 9.7 all-to-all-done.5
  929.8 12.4 convolution_convert_fusion.3
  942.2 12.1 convolution_convert_fusion.4
  954.4 8.8 convolution_convert_fusion.2
  963.2 83.0 %reduce-scatter.9.cloned.1.call-done = bf16[192,2048]{1,0:T(8,128)(2,1)} async-done(((bf16[1536,2048]{1,0:T(8,128)(2,1)}), bf16[192,2048]{1,0:T(8,128)(2,1)}) %reduce-scatter.9.cloned.1.call-update) | async-done | bytes 786448 | tf_op jit(solution)/shard_map/reduce_scatter | solution.py:293
  1047.8 6.1 fusion.60
  1053.9 35.3 %all-reduce.5 = (bf16[1536]{0:T(1024)(128)(2,1)S(1)}, bf16[2048]{0:T(1024)(128)(2,1)S(1)}, bf16[1536]{0:T(1024)(128)(2,1)S(1)}) all-reduce(bf16[1536]{0:T(1024)(128)(2,1)S(1)} %get-tuple-element.210, bf16[2048]{0:T(1024)(128)(2,1)S(1)} %fusion.75, bf16[1536]{0:T(1024)(128)(2,1)S(1)} %copy-done.29), channel_id=5, replica_groups=mesh['seq'=4,'fsdp'=8] {'fsdp'}, use_global_device_ids=true, to_apply=%region_16.17.clone | all-reduce | flops 5120 | bytes 20480
  1089.4 6.5 all-reduce.7
  1100.7 156.5 %all-reduce.11.cloned.1.call-done = (bf16[192,2048]{1,0:T(8,128)(2,1)}, bf16[192,1536]{1,0:T(8,128)(2,1)}, bf16[1120,1536]{1,0:T(8,128)(2,1)}, bf16[1120,1536]{1,0:T(8,128)(2,1)}, bf16[1120,1536]{1,0:T(8,128)(2,1)}) async-done(((bf16[192,2048]{1,0:T(8,128)(2,1)}, bf16[192,1536]{1,0:T(8,128)(2,1)}, bf16[1120,1536]{1,0:T(8,128)(2,1)}, bf16[1120,1536]{1,0:T(8,128)(2,1)}, bf16[1120,1536]{1,0:T(8,128)(2,1)}), ...) | async-done | bytes 11698192 | tf_op jit(solution)/shard_map/psum | solution.py:308
  1257.2 6.0 convert_element_type.265
  (252 shorter events, 207.4 us)
Async XLA Ops:
  7.2 427.3 %copy-start = (bf16[1120,1536]{1,0:T(8,128)(2,1)S(1)}, bf16[1120,1536]{1,0:T(8,128)(2,1)}, u32[]{:S(2)}) copy-start(bf16[1120,1536]{1,0:T(8,128)(2,1)} %param.24) | copy-start | bytes 10321924
  7.2 105.3 %all-gather.7.cloned.1.call-start = ((), (), s32[]{:S(2)}) async-start(), calls=%async_computation.12 | async-start | bytes 7077888 | tf_op jit(solution)/shard_map/all_gather | solution.py:150
  7.9 224.3 %all-gather.9.cloned.1.call-start = ((), (), s32[]{:S(2)}) async-start(), calls=%async_computation.13 | async-start | bytes 5308416 | tf_op jit(solution)/shard_map/all_gather | solution.py:152
  36.4 81.1 %copy-start.25 = (f32[1536]{0:T(1024)}, f32[1536]{0:T(1024)S(1)}, u32[]{:S(2)}) copy-start(f32[1536]{0:T(1024)S(1)} %convert_element_type.218) | copy-start | bytes 18436
  37.8 79.7 %copy-start.27 = (f32[256]{0:T(256)}, f32[256]{0:T(256)S(1)}, u32[]{:S(2)}) copy-start(f32[256]{0:T(256)S(1)} %add_rsqrt_fusion.1) | copy-start | bytes 3076
  126.3 10.1 all-to-all-start.1
  136.4 15.9 %all-to-all-start = ((bf16[256,4,384]{0,2,1:T(8,128)(2,1)}), bf16[256,4,384]{0,2,1:T(8,128)(2,1)}, u32[]{:S(2)}, u32[]{:S(2)}) async-start(bf16[256,4,384]{0,2,1:T(8,128)(2,1)} %fusion.63), calls=%async_computation | async-start | bytes 1572864 | tf_op jit(solution)/shard_map/all_to_all | solution.py:173
  154.0 12.0 all-to-all-start.2
  207.9 15.9 %all-to-all-start.3 = ((bf16[4,2,49152]{2,1,0:T(2,128)(2,1)}), bf16[4,2,49152]{2,1,0:T(2,128)(2,1)}, u32[]{:S(2)}, u32[]{:S(2)}) async-start(bf16[4,2,49152]{2,1,0:T(2,128)(2,1)} %reshape.324), calls=%async_computation.3 | async-start | bytes 1572864 | tf_op jit(solution)/shard_map/all_to_all | solution.py:181
  212.1 123.1 %all-gather.11.cloned.1.call-start = ((), (), s32[]{:S(2)}) async-start(), calls=%async_computation.14 | async-start | bytes 7077888 | tf_op jit(solution)/shard_map/all_gather | solution.py:193
  238.8 195.7 %all-gather.13.cloned.1.call-start = ((), (), s32[]{:S(2)}) async-start(), calls=%async_computation.19 | async-start | bytes 7077888 | tf_op jit(solution)/shard_map/all_gather | solution.py:203
  239.4 446.4 %reduce-scatter.7.cloned.1.call-start = ((), (), s32[]{:S(2)}) async-start(), calls=%async_computation.16 | async-start | bytes 14155776 | tf_op jit(solution)/shard_map/reduce_scatter | solution.py:214
  335.2 13.4 %copy-start.30 = (bf16[2048,1536]{1,0:T(8,128)(2,1)S(1)}, bf16[2048,1536]{1,0:T(8,128)(2,1)}, u32[]{:S(2)}) copy-start(bf16[2048,1536]{1,0:T(8,128)(2,1)} %all-gather.11.cloned.1.call-done) | copy-start | bytes 18874372
  335.2 13.4 %copy-start.32 = (bf16[1120,1536]{1,0:T(8,128)(2,1)S(1)}, bf16[1120,1536]{1,0:T(8,128)(2,1)}, u32[]{:S(2)}) copy-start(bf16[1120,1536]{1,0:T(8,128)(2,1)} %param.23) | copy-start | bytes 10321924
  434.5 18.3 %copy-start.31 = (bf16[1120,1536]{1,0:T(8,128)(2,1)S(1)}, bf16[1120,1536]{1,0:T(8,128)(2,1)}, u32[]{:S(2)}) copy-start(bf16[1120,1536]{1,0:T(8,128)(2,1)} %param.22) | copy-start | bytes 10321924
  452.8 13.0 %copy-start.33 = (bf16[1120,1536]{1,0:T(8,128)(2,1)S(1)}, bf16[1120,1536]{1,0:T(8,128)(2,1)}, u32[]{:S(2)}) copy-start(bf16[1120,1536]{1,0:T(8,128)(2,1)} %param.23) | copy-start | bytes 10321924
  452.8 13.0 %copy-start.34 = (bf16[2048,1120]{0,1:T(8,128)(2,1)S(1)}, bf16[2048,1120]{0,1:T(8,128)(2,1)}, u32[]{:S(2)}) copy-start(bf16[2048,1120]{0,1:T(8,128)(2,1)} %get-tuple-element.263) | copy-start | bytes 13762564
  480.1 326.7 %reduce-scatter.5.cloned.1.call-start = ((), (), s32[]{:S(2)}) async-start(), calls=%async_computation.15 | async-start | bytes 7077888 | tf_op jit(solution)/shard_map/reduce_scatter | solution.py:200
  492.6 193.2 %copy-start.6 = (f32[256,1536]{1,0:T(8,128)S(1)}, f32[256,1536]{1,0:T(8,128)}, u32[]{:S(2)}) copy-start(f32[256,1536]{1,0:T(8,128)} %copy-done.5) | copy-start | bytes 4718596
  810.0 9.1 copy-start.10
  815.5 15.1 %all-to-all-start.4 = ((bf16[256,4,384]{0,2,1:T(8,128)(2,1)}), bf16[256,4,384]{0,2,1:T(8,128)(2,1)S(1)}, u32[]{:S(2)}, u32[]{:S(2)}) async-start(bf16[256,4,384]{0,2,1:T(8,128)(2,1)} %bitcast.275), calls=%async_computation.6 | async-start | bytes 1572864 | tf_op jit(solution)/shard_map/all_to_all | solution.py:226
  819.0 144.1 %reduce-scatter.11.cloned.1.call-start = ((), (), s32[]{:S(2)}) async-start(), calls=%async_computation.18 | async-start | bytes 5308416 | tf_op jit(solution)/shard_map/reduce_scatter | solution.py:299
  881.5 9.4 all-to-all-start.6
  890.9 13.6 %all-to-all-start.7 = ((bf16[4,2,16384]{2,1,0:T(2,128)(2,1)}), bf16[4,2,16384]{2,1,0:T(2,128)(2,1)S(1)}, u32[]{:S(2)}, u32[]{:S(2)}) async-start(bf16[4,2,16384]{2,1,0:T(2,128)(2,1)} %reshape.326), calls=%async_computation.9 | async-start | bytes 524288 | tf_op jit(solution)/shard_map/all_to_all | solution.py:255
  904.5 15.1 %all-to-all-start.5 = ((bf16[4,2,49152]{2,1,0:T(2,128)(2,1)}), bf16[4,2,49152]{2,1,0:T(2,128)(2,1)S(1)}, u32[]{:S(2)}, u32[]{:S(2)}) async-start(bf16[4,2,49152]{2,1,0:T(2,128)(2,1)} %reshape.330), calls=%async_computation.7 | async-start | bytes 1572864 | tf_op jit(solution)/shard_map/all_to_all | solution.py:241
  908.0 138.2 %reduce-scatter.9.cloned.1.call-start = ((), (), s32[]{:S(2)}) async-start(), calls=%async_computation.17 | async-start | bytes 7077888 | tf_op jit(solution)/shard_map/reduce_scatter | solution.py:293
  929.7 327.4 %all-reduce.11.cloned.1.call-start = ((), (), s32[]{:S(2)}) async-start(), calls=%async_computation.20 | async-start | bytes 23396352 | tf_op jit(solution)/shard_map/psum | solution.py:308
  929.8 24.6 %slice-start = ((s8[6291456]{0:T(1024)(128)(4,1)}), s8[4194304]{0:T(1024)(128)(4,1)S(1)}, s32[]{:S(2)}) async-start(s8[6291456]{0:T(1024)(128)(4,1)} %bitcast.290), calls=%async_computation.21 | async-start | bytes 8388608
  929.8 24.6 %slice-start.2 = ((s8[4587520]{0:T(1024)(128)(4,1)}), s8[4194304]{0:T(1024)(128)(4,1)S(1)}, s32[]{:S(2)}) async-start(s8[4587520]{0:T(1024)(128)(4,1)} %bitcast.292), calls=%async_computation.23 | async-start | bytes 8388608
  942.2 12.2 slice-start.1
  942.2 12.2 slice-start.3
  1047.8 49.9 %copy-start.11 = (f32[256,1536]{1,0:T(8,128)S(1)}, f32[256,1536]{1,0:T(8,128)}, u32[]{:S(2)}) copy-start(f32[256,1536]{1,0:T(8,128)} %copy-done.10) | copy-start | bytes 4718596
  (29 other events, 114.3 us)
Sparse Core Ops, SparseCore 0:
  10.2 102.2 all-gather.6
  114.7 78.0 all-gather.8
  238.9 96.2 all-gather.10
  337.2 97.2 all-gather.12
  480.2 205.4 reduce-scatter.6
  689.7 117.0 reduce-scatter.4
  824.1 95.0 reduce-scatter.10
  929.8 116.2 reduce-scatter.8
  1049.7 207.3 all-reduce.10
where the time goes:
time: 1290 us; the launch traced here: 1280 us
  waiting for transfers between devices  823 us (64%)
  matrix products  191 us (15%)
  blocking collectives  82.2 us (6%)
  other arithmetic  66.4 us (5%)
  local copies, waits for them, and re-layouts  61.1 us (5%)
  starting transfers between devices  31.4 us (2%)
  between operations  16.8 us (1%)
    reduce_scatter x1, waiting for transfers between devices, per_device(): lax.psum_scatter(partial_back, 'fsdp', scatter_dimension=0, tiled=True)  193 us
    psum x1, waiting for transfers between devices, per_device(): lax.psum(shard_qkv.astype(jnp.bfloat16), 'seq').astype(jnp.float32)  156 us
    reduce_scatter x1, waiting for transfers between devices, per_device(): lax.psum_scatter(partial_out.astype(jnp.bfloat16), 'fsdp', scatter_dimens...  119 us
    all_gather x1, waiting for transfers between devices, per_device(): all_rows = lax.all_gather(normed_two, 'fsdp', axis=0, tiled=True)  95.6 us
    reduce_scatter x1, waiting for transfers between devices, per_device(): lax.psum_scatter(term_qkv.astype(jnp.bfloat16), 'fsdp', scatter_dimension...  83 us
    all_gather x1, waiting for transfers between devices, per_device(): all_grads = lax.all_gather(grad_mlp, 'fsdp', axis=0, tiled=True)  76.3 us
    unnamed x2, blocking collectives  59.2 us
    all_gather x1, waiting for transfers between devices, per_device(): lax.all_gather(qkv_weight, 'fsdp', axis=0, tiled=True)  52.2 us
  transfers between devices with their start and end apart: 17, of which 13 were waited for; matrix products, arithmetic and copies ran while one was open for 19% of the time, Pallas kernels for 0%

commit v1 on v0

--- a/solution.py
+++ b/solution.py
@@ -200,7 +200,13 @@
     mlp_out = lax.psum_scatter(
         partial_out.astype(jnp.bfloat16), "fsdp", scatter_dimension=0, tiled=True
     ).astype(jnp.float32)
-    all_grads = lax.all_gather(grad_mlp, "fsdp", axis=0, tiled=True)
+    n_dev = lax.axis_size("fsdp")
+    held, blocks = (grad_mlp, [grad_mlp])
+    for _ in range(n_dev - 1):
+        held = lax.ppermute(held, "fsdp", [(i, (i + 1) % n_dev) for i in range(n_dev)])
+        blocks.insert(0, held)
+    line = jnp.concatenate(blocks, axis=0)
+    all_grads = jnp.roll(line, (lax.axis_index("fsdp") + 1) * grad_mlp.shape[0], axis=0)
     grad_hidden = jnp.einsum(
         "tm,fm->tf", all_grads, down_weight, preferred_element_type=jnp.float32
     )

time: 1290 us -> 1340 us (1.039)
  waiting for transfers between devices: 823 us -> 851 us
  local copies, waits for them, and re-layouts: 61.1 us -> 86.5 us
    ppermute x0 -> x7, waiting for transfers between devices: none -> 201 us  [per_device(): lax.ppermute(held, 'fsdp', [(i, (i + 1) % n_dev) for i in range(n_dev)])]
    all_gather x1, waiting for transfers between devices: 95.6 us -> 0.01 us  [per_device(): all_rows = lax.all_gather(normed_two, 'fsdp', axis=0, tiled=True)]
    all_gather x1 -> x0, waiting for transfers between devices: 76.3 us -> none  [per_device(): all_grads = lax.all_gather(grad_mlp, 'fsdp', axis=0, tiled=True)]
    unnamed x87 -> x116, local copies, waits for them, and re-layouts: 20 us -> 44.3 us
  transfers between devices with their start and end apart: 17 -> 23, of which waited for: 13 -> 18; matrix products, arithmetic and copies ran while one was open for 19% -> 18% of each run, Pallas kernels for 0% -> 0%
where the time goes in v1:
time: 1340 us
  waiting for transfers between devices  851 us (64%)
  matrix products  192 us (14%)
  local copies, waits for them, and re-layouts  86.5 us (6%)
  blocking collectives  82.3 us (6%)
  other arithmetic  66.6 us (5%)
  starting transfers between devices  32 us (2%)
  between operations  17.3 us (1%)
    ppermute x7, waiting for transfers between devices, per_device(): lax.ppermute(held, 'fsdp', [(i, (i + 1) % n_dev) for i in range(n_dev)])  201 us
    reduce_scatter x1, waiting for transfers between devices, per_device(): lax.psum_scatter(partial_back, 'fsdp', scatter_dimension=0, tiled=True)  195 us
    psum x1, waiting for transfers between devices, per_device(): lax.psum(shard_qkv.astype(jnp.bfloat16), 'seq').astype(jnp.float32)  156 us
    reduce_scatter x1, waiting for transfers between devices, per_device(): lax.psum_scatter(partial_out.astype(jnp.bfloat16), 'fsdp', scatter_dimens...  119 us
    reduce_scatter x1, waiting for transfers between devices, per_device(): lax.psum_scatter(term_qkv.astype(jnp.bfloat16), 'fsdp', scatter_dimension...  79.8 us
    unnamed x2, blocking collectives  59.2 us
    all_gather x1, waiting for transfers between devices, per_device(): lax.all_gather(qkv_weight, 'fsdp', axis=0, tiled=True)  52.2 us
    unnamed x116, local copies, waits for them, and re-layouts  44.3 us
  transfers between devices with their start and end apart: 23, of which 18 were waited for; matrix products, arithmetic and copies ran while one was open for 18% of the time, Pallas kernels for 0%

profile of v1, /device:TPU:0, one launch (start us, length us, event | category | flops | bytes accessed | tf_op | source)
XLA Modules:
  0.0 1335.7 jit_solution(9731253927210930281)
XLA Ops:
  12.4 23.9 %all-reduce.6 = (bf16[1536]{0:T(1024)(128)(2,1)S(1)}, bf16[1536]{0:T(1024)(128)(2,1)S(1)}) all-reduce(bf16[1536]{0:T(1024)(128)(2,1)S(1)} %dynamic-update-slice, bf16[1536]{0:T(1024)(128)(2,1)S(1)} %dynamic-update-slice.1), channel_id=1, replica_groups=mesh['seq'=4,'fsdp'=8] {'fsdp'}, use_global_device_ids=true, to_apply=%add | all-reduce | flops 3072 | bytes 12288
  38.4 16.5 %all-gather = bf16[8,1,256]{2,1,0:T(2,128)(2,1)S(1)} all-gather(bf16[1,1,256]{2,1,0:T(2,128)(2,1)S(1)} %reshape.304), channel_id=1, replica_groups=mesh['seq'=4,'fsdp'=8] {'fsdp'}, dimensions={0}, use_global_device_ids=true | all-gather | bytes 4608 | tf_op jit(solution)/shard_map/all_gather | solution.py:151
  60.3 52.2 %all-gather.5.cloned.1.call-done = bf16[1536,2048]{1,0:T(8,128)(2,1)} async-done(((bf16[192,2048]{1,0:T(8,128)(2,1)}), bf16[1536,2048]{1,0:T(8,128)(2,1)}) %all-gather.5.cloned.1.call-update) | async-done | bytes 6291472 | tf_op jit(solution)/shard_map/all_gather | solution.py:150
  142.2 10.1 all-to-all-done
  165.9 23.9 %while.27 = (s32[]{:T(128)}, bf16[2,512,3,128]{3,1,2,0:T(8,128)(2,1)}, f32[2,3,512]{2,1,0:T(4,128)S(1)}, s32[2]{0:T(128)S(1)}, bf16[1024,3,128]{2,0,1:T(8,128)(2...) while((s32[]{:T(128)}, ...), condition=%wide.region_4.5_spmd, body=%wide.region_1.4_spmd.sunk | while | flops 824900608 | bytes 22342304 | solution.py:79
  198.7 7.3 reduce.2
  212.4 11.5 all-to-all-done.3
  239.4 33.5 %collective-permute-done = bf16[256,1536]{1,0:T(8,128)(2,1)S(1)} collective-permute-done((bf16[256,1536]{1,0:T(8,128)(2,1)}, bf16[256,1536]{1,0:T(8,128)(2,1)S(1)}, u32[]{:S(2)}, u32[]{:S(2)}) %collective-permute-start) | collective-permute-done | bytes 786464 | tf_op jit(solution)/shard_map/ppermute | solution.py:206
  273.8 29.5 %collective-permute-done.1 = bf16[256,1536]{1,0:T(8,128)(2,1)S(1)} collective-permute-done((bf16[256,1536]{1,0:T(8,128)(2,1)S(1)}, bf16[256,1536]{1,0:T(8,128)(2,1)S(1)}, u32[]{:S(2)}, u32[]{:S(2)}) %collective-permute-start.1) | collective-permute-done | bytes 786464 | tf_op jit(solution)/shard_map/ppermute | solution.py:206
  304.2 39.0 %collective-permute-done.2 = bf16[256,1536]{1,0:T(8,128)(2,1)S(1)} collective-permute-done((bf16[256,1536]{1,0:T(8,128)(2,1)S(1)}, bf16[256,1536]{1,0:T(8,128)(2,1)S(1)}, u32[]{:S(2)}, u32[]{:S(2)}) %collective-permute-start.2) | collective-permute-done | bytes 786464 | tf_op jit(solution)/shard_map/ppermute | solution.py:206
  344.1 38.8 %collective-permute-done.3 = bf16[256,1536]{1,0:T(8,128)(2,1)S(1)} collective-permute-done((bf16[256,1536]{1,0:T(8,128)(2,1)S(1)}, bf16[256,1536]{1,0:T(8,128)(2,1)S(1)}, u32[]{:S(2)}, u32[]{:S(2)}) %collective-permute-start.3) | collective-permute-done | bytes 786464 | tf_op jit(solution)/shard_map/ppermute | solution.py:206
  383.8 20.9 %collective-permute-done.4 = bf16[256,1536]{1,0:T(8,128)(2,1)S(1)} collective-permute-done((bf16[256,1536]{1,0:T(8,128)(2,1)S(1)}, bf16[256,1536]{1,0:T(8,128)(2,1)S(1)}, u32[]{:S(2)}, u32[]{:S(2)}) %collective-permute-start.4) | collective-permute-done | bytes 786464 | tf_op jit(solution)/shard_map/ppermute | solution.py:206
  405.5 20.1 %collective-permute-done.5 = bf16[256,1536]{1,0:T(8,128)(2,1)} collective-permute-done((bf16[256,1536]{1,0:T(8,128)(2,1)S(1)}, bf16[256,1536]{1,0:T(8,128)(2,1)}, u32[]{:S(2)}, u32[]{:S(2)}) %collective-permute-start.5) | collective-permute-done | bytes 786464 | tf_op jit(solution)/shard_map/ppermute | solution.py:206
  425.6 19.3 %collective-permute-done.6 = bf16[256,1536]{1,0:T(8,128)(2,1)} collective-permute-done((bf16[256,1536]{1,0:T(8,128)(2,1)}, bf16[256,1536]{1,0:T(8,128)(2,1)}, u32[]{:S(2)}, u32[]{:S(2)}) %collective-permute-start.6) | collective-permute-done | bytes 786464 | tf_op jit(solution)/shard_map/ppermute | solution.py:206
  466.0 13.0 fusion.82
  479.0 9.6 fusion.83
  488.7 18.1 %multiply_convert_fusion = (bf16[2048,1120]{0,1:T(8,128)(2,1)}, bf16[2048,1120]{0,1:T(8,128)(2,1)}, bf16[2048,1120]{0,1:T(8,128)(2,1)}) fusion(f32[2048,1120]{0,1:T(8,128)} %fusion.82, f32[2048,1120]{0,1:T(8,128)} %fusion.83, bf16[1120,1536]{1,0:T(8,128)(2,1)S(1)} %copy-done, bf16[4096,1536]{1,0:T(8,128)(2,1)} %constant_dynamic-update-slice_fusion, ...), kind=kOutput, calls=%fused_computation.56 | convolution fusion | flops 7080837120 | bytes 41844740 | tf_op jit(solution)/shard_map/tm,fm->tf/dot_general | solution.py:210
  506.8 11.7 fusion.84
  518.5 13.9 %convolution_add_fusion = f32[2048,1536]{1,0:T(8,128)} fusion(f32[2048,1536]{1,0:T(8,128)S(1)} %fusion.84, bf16[2048,1120]{0,1:T(8,128)(2,1)} %get-tuple-element.263, bf16[1120,1536]{1,0:T(8,128)(2,1)S(1)} %copy-done.45), kind=kOutput, calls=%fused_computation.61 | convolution fusion | flops 7049576448 | bytes 33193984 | tf_op jit(solution)/shard_map/dot_general | solution.py:217
  532.5 12.4 convolution_convert_fusion
  545.0 195.3 %reduce-scatter.7.cloned.1.call-done = f32[256,1536]{1,0:T(8,128)} async-done(((f32[2048,1536]{1,0:T(8,128)}), f32[256,1536]{1,0:T(8,128)}) %reduce-scatter.7.cloned.1.call-update) | async-done | bytes 1572880 | tf_op jit(solution)/shard_map/reduce_scatter | solution.py:220
  742.8 118.7 %reduce-scatter.5.cloned.1.call-done = bf16[256,1536]{1,0:T(8,128)(2,1)} async-done(((bf16[2048,1536]{1,0:T(8,128)(2,1)}), bf16[256,1536]{1,0:T(8,128)(2,1)}) %reduce-scatter.5.cloned.1.call-update) | async-done | bytes 786448 | tf_op jit(solution)/shard_map/reduce_scatter | solution.py:200
  877.4 7.9 all-to-all-done.4
  886.5 47.3 %while.28 = (s32[]{:T(128)}, f32[1024,128]{1,0:T(8,128)}, f32[1024,128]{1,0:T(8,128)}, bf16[2,512,3,128]{3,1,2,0:T(8,128)(2,1)}, s32[2]{0:T(128)S(1)}, /*index=5...) while((s32[]{:T(128)}, f32[1024,128]{1,0:T(8,128)}, ...), condition=%wide.region_11.12_spmd.clone, body=%wide.region_9.11_spmd.clone.sunk | while | flops 2038234112 | bytes 90227544 | solution.py:120
  965.2 9.7 all-to-all-done.5
  984.9 12.3 convolution_convert_fusion.2
  997.2 12.1 convolution_convert_fusion.3
  1009.3 12.0 convolution_convert_fusion.4
  1021.3 79.8 %reduce-scatter.9.cloned.1.call-done = bf16[192,2048]{1,0:T(8,128)(2,1)} async-done(((bf16[1536,2048]{1,0:T(8,128)(2,1)}), bf16[192,2048]{1,0:T(8,128)(2,1)}) %reduce-scatter.9.cloned.1.call-update) | async-done | bytes 786448 | tf_op jit(solution)/shard_map/reduce_scatter | solution.py:299
  1109.0 35.3 %all-reduce.5 = (bf16[1536]{0:T(1024)(128)(2,1)S(1)}, bf16[2048]{0:T(1024)(128)(2,1)S(1)}, bf16[1536]{0:T(1024)(128)(2,1)S(1)}) all-reduce(bf16[1536]{0:T(1024)(128)(2,1)S(1)} %get-tuple-element.210, bf16[2048]{0:T(1024)(128)(2,1)S(1)} %fusion.77, bf16[1536]{0:T(1024)(128)(2,1)S(1)} %copy-done.42), channel_id=4, replica_groups=mesh['seq'=4,'fsdp'=8] {'fsdp'}, use_global_device_ids=true, to_apply=%region_16.17.clone | all-reduce | flops 5120 | bytes 20480
  1144.5 6.5 all-reduce.7
  1155.7 156.5 %all-reduce.11.cloned.1.call-done = (bf16[192,2048]{1,0:T(8,128)(2,1)}, bf16[192,1536]{1,0:T(8,128)(2,1)}, bf16[1120,1536]{1,0:T(8,128)(2,1)}, bf16[1120,1536]{1,0:T(8,128)(2,1)}, bf16[1120,1536]{1,0:T(8,128)(2,1)}) async-done(((bf16[192,2048]{1,0:T(8,128)(2,1)}, bf16[192,1536]{1,0:T(8,128)(2,1)}, bf16[1120,1536]{1,0:T(8,128)(2,1)}, bf16[1120,1536]{1,0:T(8,128)(2,1)}, bf16[1120,1536]{1,0:T(8,128)(2,1)}), ...) | async-done | bytes 11698192 | tf_op jit(solution)/shard_map/psum | solution.py:314
  (291 shorter events, 262.8 us)
Async XLA Ops:
  7.2 481.5 %copy-start = (bf16[1120,1536]{1,0:T(8,128)(2,1)S(1)}, bf16[1120,1536]{1,0:T(8,128)(2,1)}, u32[]{:S(2)}) copy-start(bf16[1120,1536]{1,0:T(8,128)(2,1)} %param.24) | copy-start | bytes 10321924
  7.2 105.3 %all-gather.5.cloned.1.call-start = ((), (), s32[]{:S(2)}) async-start(), calls=%async_computation.12 | async-start | bytes 7077888 | tf_op jit(solution)/shard_map/all_gather | solution.py:150
  7.9 224.3 %all-gather.7.cloned.1.call-start = ((), (), s32[]{:S(2)}) async-start(), calls=%async_computation.13 | async-start | bytes 5308416 | tf_op jit(solution)/shard_map/all_gather | solution.py:152
  36.4 81.1 %copy-start.38 = (f32[1536]{0:T(1024)}, f32[1536]{0:T(1024)S(1)}, u32[]{:S(2)}) copy-start(f32[1536]{0:T(1024)S(1)} %convert_element_type.218) | copy-start | bytes 18436
  37.8 79.7 %copy-start.40 = (f32[256]{0:T(256)}, f32[256]{0:T(256)S(1)}, u32[]{:S(2)}) copy-start(f32[256]{0:T(256)S(1)} %add_rsqrt_fusion.1) | copy-start | bytes 3076
  126.3 10.1 all-to-all-start.1
  136.4 15.9 %all-to-all-start = ((bf16[256,4,384]{0,2,1:T(8,128)(2,1)}), bf16[256,4,384]{0,2,1:T(8,128)(2,1)}, u32[]{:S(2)}, u32[]{:S(2)}) async-start(bf16[256,4,384]{0,2,1:T(8,128)(2,1)} %fusion.63), calls=%async_computation | async-start | bytes 1572864 | tf_op jit(solution)/shard_map/all_to_all | solution.py:173
  154.0 12.0 all-to-all-start.2
  207.9 15.9 %all-to-all-start.3 = ((bf16[4,2,49152]{2,1,0:T(2,128)(2,1)}), bf16[4,2,49152]{2,1,0:T(2,128)(2,1)}, u32[]{:S(2)}, u32[]{:S(2)}) async-start(bf16[4,2,49152]{2,1,0:T(2,128)(2,1)} %reshape.322), calls=%async_computation.3 | async-start | bytes 1572864 | tf_op jit(solution)/shard_map/all_to_all | solution.py:181
  212.1 253.9 %all-gather.9.cloned.1.call-start = ((), (), s32[]{:S(2)}) async-start(), calls=%async_computation.14 | async-start | bytes 7077888 | tf_op jit(solution)/shard_map/all_gather | solution.py:193
  238.8 501.5 %reduce-scatter.7.cloned.1.call-start = ((), (), s32[]{:S(2)}) async-start(), calls=%async_computation.16 | async-start | bytes 14155776 | tf_op jit(solution)/shard_map/reduce_scatter | solution.py:220
  238.8 34.0 %collective-permute-start = (bf16[256,1536]{1,0:T(8,128)(2,1)}, bf16[256,1536]{1,0:T(8,128)(2,1)S(1)}, u32[]{:S(2)}, u32[]{:S(2)}) collective-permute-start(bf16[256,1536]{1,0:T(8,128)(2,1)} %bitcast.266), channel_id=1, source_target_pairs={{0,1},{1,2},{2,3},{3,4},{4,5},{5,6},{6,7},{7,0},{8,9},{9,10},{10,1... | collective-permute-start | bytes 2359304 | tf_op jit(solution)/shard_map/ppermute | solution.py:206
  273.8 29.5 %collective-permute-start.1 = (bf16[256,1536]{1,0:T(8,128)(2,1)S(1)}, bf16[256,1536]{1,0:T(8,128)(2,1)S(1)}, u32[]{:S(2)}, u32[]{:S(2)}) collective-permute-start(bf16[256,1536]{1,0:T(8,128)(2,1)S(1)} %collective-permute-done), channel_id=1, source_target_pairs={{0,1},{1,2},{2,3},{3,4},{4,5},{5,6},{6,7},{7,0},{8,9},{9,10},{10,1... | collective-permute-start | bytes 2359304 | tf_op jit(solution)/shard_map/ppermute | solution.py:206
  304.2 39.0 %collective-permute-start.2 = (bf16[256,1536]{1,0:T(8,128)(2,1)S(1)}, bf16[256,1536]{1,0:T(8,128)(2,1)S(1)}, u32[]{:S(2)}, u32[]{:S(2)}) collective-permute-start(bf16[256,1536]{1,0:T(8,128)(2,1)S(1)} %collective-permute-done.1), channel_id=1, source_target_pairs={{0,1},{1,2},{2,3},{3,4},{4,5},{5,6},{6,7},{7,0},{8,9},{9,10},{10,1... | collective-permute-start | bytes 2359304 | tf_op jit(solution)/shard_map/ppermute | solution.py:206
  344.1 38.8 %collective-permute-start.3 = (bf16[256,1536]{1,0:T(8,128)(2,1)S(1)}, bf16[256,1536]{1,0:T(8,128)(2,1)S(1)}, u32[]{:S(2)}, u32[]{:S(2)}) collective-permute-start(bf16[256,1536]{1,0:T(8,128)(2,1)S(1)} %collective-permute-done.2), channel_id=1, source_target_pairs={{0,1},{1,2},{2,3},{3,4},{4,5},{5,6},{6,7},{7,0},{8,9},{9,10},{10,1... | collective-permute-start | bytes 2359304 | tf_op jit(solution)/shard_map/ppermute | solution.py:206
  383.8 20.9 %collective-permute-start.4 = (bf16[256,1536]{1,0:T(8,128)(2,1)S(1)}, bf16[256,1536]{1,0:T(8,128)(2,1)S(1)}, u32[]{:S(2)}, u32[]{:S(2)}) collective-permute-start(bf16[256,1536]{1,0:T(8,128)(2,1)S(1)} %collective-permute-done.3), channel_id=1, source_target_pairs={{0,1},{1,2},{2,3},{3,4},{4,5},{5,6},{6,7},{7,0},{8,9},{9,10},{10,1... | collective-permute-start | bytes 2359304 | tf_op jit(solution)/shard_map/ppermute | solution.py:206
  405.5 20.1 %collective-permute-start.5 = (bf16[256,1536]{1,0:T(8,128)(2,1)S(1)}, bf16[256,1536]{1,0:T(8,128)(2,1)}, u32[]{:S(2)}, u32[]{:S(2)}) collective-permute-start(bf16[256,1536]{1,0:T(8,128)(2,1)S(1)} %collective-permute-done.4), channel_id=1, source_target_pairs={{0,1},{1,2},{2,3},{3,4},{4,5},{5,6},{6,7},{7,0},{8,9},{9,10},{10,1... | collective-permute-start | bytes 2359304 | tf_op jit(solution)/shard_map/ppermute | solution.py:206
  425.6 19.4 %collective-permute-start.6 = (bf16[256,1536]{1,0:T(8,128)(2,1)}, bf16[256,1536]{1,0:T(8,128)(2,1)}, u32[]{:S(2)}, u32[]{:S(2)}) collective-permute-start(bf16[256,1536]{1,0:T(8,128)(2,1)} %collective-permute-done.5), channel_id=1, source_target_pairs={{0,1},{1,2},{2,3},{3,4},{4,5},{5,6},{6,7},{7,0},{8,9},{9,10},{10,1... | collective-permute-start | bytes 2359304 | tf_op jit(solution)/shard_map/ppermute | solution.py:206
  425.6 25.7 %copy-start.24 = (bf16[256,1536]{1,0:T(8,128)(2,1)S(1)}, bf16[256,1536]{1,0:T(8,128)(2,1)}, u32[]{:S(2)}) copy-start(bf16[256,1536]{1,0:T(8,128)(2,1)} %copy-done.23) | copy-start | bytes 2359300
  425.6 26.6 %copy-start.22 = (bf16[256,1536]{1,0:T(8,128)(2,1)S(1)}, bf16[256,1536]{1,0:T(8,128)(2,1)}, u32[]{:S(2)}) copy-start(bf16[256,1536]{1,0:T(8,128)(2,1)} %copy-done.21) | copy-start | bytes 2359300
  425.6 27.6 %copy-start.20 = (bf16[256,1536]{1,0:T(8,128)(2,1)S(1)}, bf16[256,1536]{1,0:T(8,128)(2,1)}, u32[]{:S(2)}) copy-start(bf16[256,1536]{1,0:T(8,128)(2,1)} %copy-done.19) | copy-start | bytes 2359300
  425.6 28.5 %copy-start.18 = (bf16[256,1536]{1,0:T(8,128)(2,1)S(1)}, bf16[256,1536]{1,0:T(8,128)(2,1)}, u32[]{:S(2)}) copy-start(bf16[256,1536]{1,0:T(8,128)(2,1)} %copy-done.17) | copy-start | bytes 2359300
  532.5 329.0 %reduce-scatter.5.cloned.1.call-start = ((), (), s32[]{:S(2)}) async-start(), calls=%async_computation.15 | async-start | bytes 7077888 | tf_op jit(solution)/shard_map/reduce_scatter | solution.py:200
  544.9 195.4 %copy-start.6 = (f32[256,1536]{1,0:T(8,128)S(1)}, f32[256,1536]{1,0:T(8,128)}, u32[]{:S(2)}) copy-start(f32[256,1536]{1,0:T(8,128)} %copy-done.5) | copy-start | bytes 4718596
  870.2 15.1 %all-to-all-start.4 = ((bf16[256,4,384]{0,2,1:T(8,128)(2,1)}), bf16[256,4,384]{0,2,1:T(8,128)(2,1)S(1)}, u32[]{:S(2)}, u32[]{:S(2)}) async-start(bf16[256,4,384]{0,2,1:T(8,128)(2,1)} %bitcast.270), calls=%async_computation.6 | async-start | bytes 1572864 | tf_op jit(solution)/shard_map/all_to_all | solution.py:232
  873.7 147.6 %reduce-scatter.11.cloned.1.call-start = ((), (), s32[]{:S(2)}) async-start(), calls=%async_computation.18 | async-start | bytes 5308416 | tf_op jit(solution)/shard_map/reduce_scatter | solution.py:305
  936.7 9.4 all-to-all-start.6
  946.1 13.6 %all-to-all-start.7 = ((bf16[4,2,16384]{2,1,0:T(2,128)(2,1)}), bf16[4,2,16384]{2,1,0:T(2,128)(2,1)S(1)}, u32[]{:S(2)}, u32[]{:S(2)}) async-start(bf16[4,2,16384]{2,1,0:T(2,128)(2,1)} %reshape.324), calls=%async_computation.9 | async-start | bytes 524288 | tf_op jit(solution)/shard_map/all_to_all | solution.py:261
  959.7 15.1 %all-to-all-start.5 = ((bf16[4,2,49152]{2,1,0:T(2,128)(2,1)}), bf16[4,2,49152]{2,1,0:T(2,128)(2,1)S(1)}, u32[]{:S(2)}, u32[]{:S(2)}) async-start(bf16[4,2,49152]{2,1,0:T(2,128)(2,1)} %reshape.328), calls=%async_computation.7 | async-start | bytes 1572864 | tf_op jit(solution)/shard_map/all_to_all | solution.py:247
  963.3 137.9 %reduce-scatter.9.cloned.1.call-start = ((), (), s32[]{:S(2)}) async-start(), calls=%async_computation.17 | async-start | bytes 7077888 | tf_op jit(solution)/shard_map/reduce_scatter | solution.py:299
  984.9 327.3 %all-reduce.11.cloned.1.call-start = ((), (), s32[]{:S(2)}) async-start(), calls=%async_computation.19 | async-start | bytes 23396352 | tf_op jit(solution)/shard_map/psum | solution.py:314
  1102.8 49.9 %copy-start.11 = (f32[256,1536]{1,0:T(8,128)S(1)}, f32[256,1536]{1,0:T(8,128)}, u32[]{:S(2)}) copy-start(f32[256,1536]{1,0:T(8,128)} %copy-done.10) | copy-start | bytes 4718596
  (42 other events, 244.1 us)
Sparse Core Ops, SparseCore 0:
  10.2 102.2 all-gather.4
  114.7 78.0 all-gather.6
  238.9 140.2 all-gather.8
  532.6 207.6 reduce-scatter.6
  744.3 117.0 reduce-scatter.4
  878.4 94.8 reduce-scatter.10
  985.0 116.1 reduce-scatter.8
  1104.7 207.4 all-reduce.10
